TPU v7x, 32 devices: a whole 2x2x4 slice. The times are simulated.
32 devices in a mesh: group: 4 (over x, core), shard: 8 (over z, y).
Axes of the slice: x: 2, y: 2, z: 4, core: 2. Of those that a mesh axis runs over, the one named last changes fastest.
Arguments:
- hidden: bfloat16 [8192, 768], P(('group', 'shard')), may hold values from -40 to 40
- out_grads: bfloat16 [5, 8192, 768], P(None, ('group', 'shard')), may hold values from -40 to 40
- global_inputs: bfloat16 [1024, 768], P(('group', 'shard')), may hold values from -40 to 40
- query_grads: bfloat16 [1024, 768], P(('group', 'shard')), may hold values from -40 to 40
- weight_grads: bfloat16 [6, 768, 768], P(None, 'shard'), may hold values from -48 to 48
- momentum: float32 [6, 768, 768], P(None, 'shard', 'group'), may hold values from -6 to 6
Outputs:
- new_momentum: float32 [6, 768, 768], P(None, 'shard', 'group')
All inputs are finite; a program needn't handle non-finite values. Where the computation divides by a largest or mean magnitude, that divisor is 1e-20 or more.
Results may differ from a plain program's by a relative error of at most 0.0018.
Values may be sent and summed in bfloat16 or wider, within the bound.
A program may use at most 128 MiB of HBM per device.

v0:
```python
import jax
import jax.numpy as jnp
from jax import lax
from jax.sharding import PartitionSpec as P

ITERS = 3
PRECISE = lax.Precision.HIGHEST
DAMPING = 0.1
MOMENTUM = 0.9


def broadcast(array, axis, root):
    mine = lax.axis_index(axis) == root
    return lax.psum(jnp.where(mine, array, jnp.zeros_like(array)), axis)


def outer_sum(matrix_rows):
    return lax.dot_general(
        matrix_rows, matrix_rows, (((0,), (0,)), ((), ())), preferred_element_type=jnp.float32
    )


def on_device(hidden, out_grads, global_inputs, query_grads, weight_grads, momentum):
    model_width = hidden.shape[1]
    group_size = lax.axis_size("group")
    shard_size = lax.axis_size("shard")
    per_group = 8 // group_size
    row_block = model_width // shard_size
    col_block = momentum.shape[2]
    shard_pos = lax.axis_index("shard")
    group_pos = lax.axis_index("group")
    devices = group_size * shard_size
    partials = [outer_sum(hidden), outer_sum(global_inputs)]
    partials = partials + [outer_sum(out_grads[member]) for member in range(5)]
    partials = partials + [outer_sum(query_grads)]
    stacked = jnp.stack([single.astype(jnp.bfloat16) for single in partials])
    summed = lax.psum_scatter(stacked, "group", scatter_dimension=0, tiled=True).astype(jnp.float32)
    factor_ids = group_pos * per_group + jnp.arange(per_group)
    is_global = (factor_ids == 1) | (factor_ids == 7)
    samp_total = float(hidden.shape[0] * devices)
    glob_total = float(global_inputs.shape[0] * devices)
    counted = jnp.where(is_global, glob_total, samp_total).astype(jnp.float32)
    factor_full = lax.psum(summed, "shard")
    covariance = factor_full / counted[:, None, None]
    mean_diag = jnp.trace(covariance, axis1=1, axis2=2) / model_width
    eye_full = jnp.eye(model_width, dtype=jnp.float32)
    matrix = covariance / mean_diag[:, None, None] + DAMPING * eye_full
    row_limit = jnp.max(jnp.sum(jnp.abs(matrix), axis=2), axis=1)
    approx = jnp.broadcast_to(eye_full, matrix.shape) / row_limit[:, None, None]
    for iteration in range(ITERS):
        product = jnp.einsum("kij,kjl->kil", matrix, approx, precision=PRECISE)
        approx = 2.0 * approx - jnp.einsum("kij,kjl->kil", approx, product, precision=PRECISE)
    own_rows = lax.dynamic_slice_in_dim(approx, shard_pos * row_block, row_block, 1)
    all_rows = lax.all_gather(own_rows, "group", axis=0, tiled=True)
    input_inv = jnp.stack(
        [broadcast(approx[factor % per_group], "group", factor // per_group) for factor in range(2)]
    )
    input_cols = lax.dynamic_slice_in_dim(input_inv, group_pos * col_block, col_block, 2)
    out_inverse = all_rows[2:8]
    initial = jnp.zeros(out_inverse.shape, jnp.float32)
    gathered = lax.all_gather(weight_grads, "shard", axis=1, tiled=True)
    columns = lax.slice_in_dim(out_inverse, 0, gathered.shape[1], axis=2)
    left_side = initial + jnp.einsum(
        "wrn,wnd->wrd", columns, gathered.astype(jnp.float32), precision=PRECISE
    )
    local_part = jnp.einsum("wrd,de->wre", left_side[0:5], input_cols[0], precision=PRECISE)
    global_part = jnp.dot(left_side[5], input_cols[1], precision=PRECISE)[None]
    return MOMENTUM * momentum + jnp.concatenate([local_part, global_part], axis=0)


def solution(mesh):
    placed = (
        P(("group", "shard"), None),
        P(None, ("group", "shard"), None),
        P(("group", "shard"), None),
        P(("group", "shard"), None),
        P(None, "shard", None),
        P(None, "shard", "group"),
    )
    return jax.shard_map(
        on_device, mesh=mesh, in_specs=placed, out_specs=P(None, "shard", "group"), check_vma=False
    )
```

profile of v0, /device:TPU:0, one launch (start us, length us, event | category | flops | bytes accessed | tf_op | source)
XLA Modules:
  0.0 529.7 jit_solution(5312361933273675997)
XLA Ops:
  7.4 1.0 copy-done
  8.4 1.5 fusion.14
  9.9 2.4 fusion.10
  12.3 2.7 fusion.16
  15.0 1.6 fusion.18
  16.6 1.6 fusion.20
  18.1 1.6 fusion.22
  19.7 1.5 fusion.24
  21.2 1.6 fusion.12
  23.3 1.5 fusion.26
  24.8 79.3 %reduce-scatter.2.cloned.1.call-done = bf16[2,768,768]{2,1,0:T(8,128)(2,1)} async-done(((bf16[8,768,768]{2,1,0:T(8,128)(2,1)}), bf16[2,768,768]{2,1,0:T(8,128)(2,1)}) %reduce-scatter.2.cloned.1.call-update) | async-done | bytes 2359312 | tf_op jit(solution)/shard_map/reduce_scatter | solution.py:37
  104.1 187.7 %all-reduce.5 = f32[2,768,768]{2,1,0:T(8,128)} all-reduce(bf16[2,768,768]{2,1,0:T(8,128)(2,1)} %reduce-scatter.2.cloned.1.call-done), channel_id=1, replica_groups=mesh['group'=4,'shard'=8] {'shard'}, use_global_device_ids=true, to_apply=%region_1.2 | all-reduce | flops 1179648 | bytes 7077888 | tf_op jit(solution)/shard_map/psum | solution.py:43
  291.9 3.7 select_reduce_fusion
  295.6 3.0 abs_reduce_fusion
  298.7 15.6 %fusion.2 = f32[2,768,768]{2,1,0:T(8,128)S(1)} fusion(f32[2,768,768]{2,1,0:T(8,128)} %get-tuple-element.8, f32[2]{0:T(128)S(1)} %reduce_max.9, f32[768,768]{1,0:T(8,128)} %fusion.26), kind=kOutput, calls=%fused_computation.10 | convolution fusion | flops 10872815616 | bytes 11796488 | tf_op jit(solution)/shard_map/kij,kjl->kil/dot_general | solution.py:51
  314.3 12.8 %multiply_subtract_fusion.2 = f32[2,768,768]{2,1,0:T(8,128)S(1)} fusion(f32[2]{0:T(128)S(1)} %reduce_max.9, f32[768,768]{1,0:T(8,128)S(1)} %copy-done.4, f32[2,768,768]{2,1,0:T(8,128)S(1)} %fusion.2), kind=kOutput, calls=%fused_computation.4 | convolution fusion | flops 10876354560 | bytes 11796488 | tf_op jit(solution)/shard_map/kij,kjl->kil/dot_general | solution.py:52
  327.2 12.1 %fusion.40 = f32[2,768,768]{2,1,0:T(8,128)S(1)} fusion(f32[2,768,768]{2,1,0:T(8,128)S(1)} %bitcast.80, f32[2,768,768]{2,1,0:T(8,128)S(1)} %multiply_subtract_fusion.2), kind=kOutput, calls=%fused_computation.65 | convolution fusion | flops 10871635968 | bytes 14155776 | tf_op jit(solution)/shard_map/kij,kjl->kil/dot_general | solution.py:51
  339.3 12.7 %multiply_subtract_fusion.1 = f32[2,768,768]{2,1,0:T(8,128)S(1)} fusion(f32[2,768,768]{2,1,0:T(8,128)S(1)} %multiply_subtract_fusion.2, f32[2,768,768]{2,1,0:T(8,128)S(1)} %fusion.40), kind=kOutput, calls=%fused_computation.3 | convolution fusion | flops 10873995264 | bytes 14155776 | tf_op jit(solution)/shard_map/kij,kjl->kil/dot_general | solution.py:52
  352.0 12.3 %fusion.41 = f32[2,768,768]{2,1,0:T(8,128)S(1)} fusion(f32[2,768,768]{2,1,0:T(8,128)S(1)} %bitcast.80, f32[2,768,768]{2,1,0:T(8,128)S(1)} %multiply_subtract_fusion.1), kind=kOutput, calls=%fused_computation.66 | convolution fusion | flops 10871635968 | bytes 14155776 | tf_op jit(solution)/shard_map/kij,kjl->kil/dot_general | solution.py:51
  364.3 12.5 %multiply_subtract_fusion = f32[2,768,768]{2,1,0:T(8,128)S(1)} fusion(f32[2,768,768]{2,1,0:T(8,128)S(1)} %multiply_subtract_fusion.1, f32[2,768,768]{2,1,0:T(8,128)S(1)} %fusion.41), kind=kOutput, calls=%fused_computation.2 | convolution fusion | flops 10873995264 | bytes 14155776 | tf_op jit(solution)/shard_map/kij,kjl->kil/dot_general | solution.py:52
  376.8 2.6 slice_select_fusion
  379.4 1.0 copy-done.3
  380.5 0.5 all-gather.5.cloned.1.call-update
  381.1 1.9 constant_dynamic-slice_fusion
  383.1 89.3 %all-reduce.4.cloned.1.call-done = (f32[1,768,768]{2,1,0:T(8,128)}, f32[1,768,768]{2,1,0:T(8,128)}) async-done(((f32[1,768,768]{2,1,0:T(8,128)}, f32[1,768,768]{2,1,0:T(8,128)}), (f32[1,768,768]{2,1,0:T(8,128)}, f32[1,768,768]{2,1,0:T(8,128)})) %all-reduce.4.cloned.1.call-update) | async-done | bytes 4718608 | tf_op jit(solution)/shard_map/psum | solution.py:14
  472.4 2.1 fusion.8
  474.5 14.5 %all-gather.5.cloned.1.call-done = bf16[6,768,768]{2,1,0:T(8,128)(2,1)} async-done(((bf16[6,96,768]{2,1,0:T(8,128)(2,1)}), bf16[6,768,768]{2,1,0:T(8,128)(2,1)}) %all-gather.5.cloned.1.call-update) | async-done | bytes 7077904 | tf_op jit(solution)/shard_map/all_gather | solution.py:61
  489.0 23.5 %all-gather.3.cloned.1.call-done = f32[8,96,768]{2,1,0:T(8,128)} async-done(((f32[2,96,768]{2,1,0:T(8,128)}), f32[8,96,768]{2,1,0:T(8,128)}) %all-gather.3.cloned.1.call-update) | async-done | bytes 2359312 | tf_op jit(solution)/shard_map/all_gather | solution.py:54
  512.5 6.7 %fusion.42 = f32[6,96,768]{2,1,0:T(8,128)S(1)} fusion(f32[8,96,768]{2,1,0:T(8,128)} %all-gather.3.cloned.1.call-done, bf16[6,768,768]{2,1,0:T(8,128)(2,1)} %all-gather.5.cloned.1.call-done), kind=kOutput, calls=%fused_computation.67 | convolution fusion | flops 4076863488 | bytes 11206656 | tf_op jit(solution)/shard_map/wrn,wnd->wrd/dot_general | solution.py:63
  519.3 1.3 fusion.29
  520.6 0.5 convolution_bitcast_fusion
  521.1 0.9 maximum_add_fusion
  (31 shorter events, 0.8 us)
Async XLA Ops:
  7.4 1.0 copy-start
  7.4 7.6 %copy-start.7 = (bf16[5,256,768]{2,1,0:T(8,128)(2,1)S(1)}, bf16[5,256,768]{2,1,0:T(8,128)(2,1)}, u32[]{:S(2)}) copy-start(bf16[5,256,768]{2,1,0:T(8,128)(2,1)} %param.7) | copy-start | bytes 5898244
  7.4 96.8 %reduce-scatter.2.cloned.1.call-start = ((), (), s32[]{:S(2)}) async-start(), calls=%async_computation.1 | async-start | bytes 11796480 | tf_op jit(solution)/shard_map/reduce_scatter | solution.py:37
  12.3 8.9 %copy-start.6 = (bf16[32,768]{1,0:T(8,128)(2,1)S(1)}, bf16[32,768]{1,0:T(8,128)(2,1)}, u32[]{:S(2)}) copy-start(bf16[32,768]{1,0:T(8,128)(2,1)} %param.9) | copy-start | bytes 147460
  22.9 449.5 %all-reduce.4.cloned.1.call-start = ((), (), s32[]{:S(2)}) async-start(), calls=%async_computation.4 | async-start | bytes 9437184 | tf_op jit(solution)/shard_map/psum | solution.py:14
  291.9 3.8 copy-start.2
  298.7 15.6 %copy-start.4 = (f32[768,768]{1,0:T(8,128)S(1)}, f32[768,768]{1,0:T(8,128)}, u32[]{:S(2)}) copy-start(f32[768,768]{1,0:T(8,128)} %fusion.26) | copy-start | bytes 7077892
  298.7 28.4 %slice-start = ((s8[4718592]{0:T(1024)(128)(4,1)}), s8[4194304]{0:T(1024)(128)(4,1)S(1)}, s32[]{:S(2)}) async-start(s8[4718592]{0:T(1024)(128)(4,1)} %bitcast.79), calls=%async_computation.5 | async-start | bytes 8388608
  314.3 12.9 %slice-start.1 = ((s8[4718592]{0:T(1024)(128)(4,1)}), s8[524288]{0:T(1024)(128)(4,1)S(1)}, s32[]{:S(2)}) async-start(s8[4718592]{0:T(1024)(128)(4,1)} %bitcast.79), calls=%async_computation.6 | async-start | bytes 1048576
  376.8 3.6 copy-start.3
  380.5 108.5 %all-gather.5.cloned.1.call-start = ((), (), s32[]{:S(2)}) async-start(), calls=%async_computation.3 | async-start | bytes 7962624 | tf_op jit(solution)/shard_map/all_gather | solution.py:61
  381.1 131.4 %all-gather.3.cloned.1.call-start = ((), (), s32[]{:S(2)}) async-start(), calls=%async_computation.2 | async-start | bytes 2949120 | tf_op jit(solution)/shard_map/all_gather | solution.py:54
  474.5 46.7 %copy-start.5 = (f32[6,96,192]{2,1,0:T(8,128)S(1)}, f32[6,96,192]{2,1,0:T(8,128)}, u32[]{:S(2)}) copy-start(f32[6,96,192]{2,1,0:T(8,128)} %param.11) | copy-start | bytes 1327108
  512.5 9.5 %copy-start.1 = (bf16[256,768]{1,0:T(8,128)(2,1)S(1)}, bf16[256,768]{1,0:T(8,128)(2,1)}, u32[]{:S(2)}) copy-start(bf16[256,768]{1,0:T(8,128)(2,1)} %param.6) | copy-start | bytes 1179652
Sparse Core Ops, SparseCore 0:
  23.0 81.1 reduce-scatter.1
  380.6 91.7 all-reduce.3
Sparse Core Ops, SparseCore 1:
  383.2 105.8 all-gather.4
  490.4 22.1 all-gather.2
where the time goes:
time: 534 us; the launch traced here: 530 us
  waiting for transfers between devices  207 us (39%)
  blocking collectives  188 us (35%)
  matrix products  101 us (19%)
  between operations  15.3 us (3%)
  other arithmetic  14.3 us (3%)
    psum x1, blocking collectives, on_device(): factor_full = lax.psum(summed, 'shard')  188 us
    psum x1, waiting for transfers between devices, broadcast(): return lax.psum(jnp.where(mine, array, jnp.zeros_like(array)), axis)  89.3 us
    reduce_scatter x1, waiting for transfers between devices, on_device(): lax.psum_scatter(stacked, 'group', scatter_dimension=0, tiled=True)  79.3 us
    dot_general x3, matrix products, on_device(): product = jnp.einsum('kij,kjl->kil', matrix, approx, precision=PRECISE)  39.9 us
    dot_general x3, matrix products, on_device(): jnp.einsum('kij,kjl->kil', approx, product, precision=PRECISE)  38.1 us
    all_gather x1, waiting for transfers between devices, on_device(): all_rows = lax.all_gather(own_rows, 'group', axis=0, tiled=True)  23.5 us
    all_gather x1, waiting for transfers between devices, on_device(): gathered = lax.all_gather(weight_grads, 'shard', axis=1, tiled=True)  14.5 us
    dot_general x8, matrix products, outer_sum(): lax.dot_general(matrix_rows, matrix_rows, (((0,), (0,)), ((), ())), prefe...  14.5 us
  transfers between devices with their start and end apart: 4, of which 4 were waited for; matrix products, arithmetic and copies ran while one was open for 1% of the time, Pallas kernels for 0%

commit v1 on v0

--- a/solution.py
+++ b/solution.py
@@ -1,3 +1,4 @@
+import functools
 import jax
 import jax.numpy as jnp
 from jax import lax
@@ -7,6 +8,21 @@
 PRECISE = lax.Precision.HIGHEST
 DAMPING = 0.1
 MOMENTUM = 0.9
+
+
+def fix_positions(x_local, mesh_name):
+    axis_total = jax.lax.psum(1, mesh_name)
+    upper, k_now = (x_local, 0)
+    while 1 << k_now < axis_total:
+        big = jax.lax.ppermute(
+            upper, mesh_name, perm=[(q, q ^ 1 << k_now) for q in range(axis_total)]
+        )
+        upper = upper + big
+        k_now = k_now + 1
+    return upper
+
+
+wait_words = functools.partial(fix_positions, mesh_name="shard")
 
 
 def broadcast(array, axis, root):
@@ -40,7 +56,7 @@
     samp_total = float(hidden.shape[0] * devices)
     glob_total = float(global_inputs.shape[0] * devices)
     counted = jnp.where(is_global, glob_total, samp_total).astype(jnp.float32)
-    factor_full = lax.psum(summed, "shard")
+    factor_full = wait_words(summed)
     covariance = factor_full / counted[:, None, None]
     mean_diag = jnp.trace(covariance, axis1=1, axis2=2) / model_width
     eye_full = jnp.eye(model_width, dtype=jnp.float32)

time: 534 us -> 764 us (1.43)
  waiting for transfers between devices: 207 us -> 616 us
  blocking collectives: 188 us -> 0 us
    ppermute x0 -> x3, waiting for transfers between devices: none -> 404 us  [fix_positions(): jax.lax.ppermute(upper, mesh_name, perm=[(q, q ^ 1 << k_now) for q in ran...]
    psum x1 -> x0, blocking collectives: 188 us -> none  [on_device(): factor_full = lax.psum(summed, 'shard')]
  transfers between devices with their start and end apart: 4 -> 7, of which waited for: 4 -> 7; matrix products, arithmetic and copies ran while one was open for 1% -> 1% of each run, Pallas kernels for 0% -> 0%
where the time goes in v1:
time: 764 us; the launch traced here: 761 us
  waiting for transfers between devices  616 us (81%)
  matrix products  99.8 us (13%)
  other arithmetic  20 us (3%)
  between operations  15.3 us (2%)
    ppermute x3, waiting for transfers between devices, fix_positions(): jax.lax.ppermute(upper, mesh_name, perm=[(q, q ^ 1 << k_now) for q in ran...  404 us
    psum x1, waiting for transfers between devices, broadcast(): return lax.psum(jnp.where(mine, array, jnp.zeros_like(array)), axis)  91.8 us
    reduce_scatter x1, waiting for transfers between devices, on_device(): lax.psum_scatter(stacked, 'group', scatter_dimension=0, tiled=True)  80.8 us
    dot_general x3, matrix products, on_device(): product = jnp.einsum('kij,kjl->kil', matrix, approx, precision=PRECISE)  38.8 us
    dot_general x3, matrix products, on_device(): jnp.einsum('kij,kjl->kil', approx, product, precision=PRECISE)  38 us
    all_gather x1, waiting for transfers between devices, on_device(): all_rows = lax.all_gather(own_rows, 'group', axis=0, tiled=True)  23.5 us
  transfers between devices with their start and end apart: 7, of which 7 were waited for; matrix products, arithmetic and copies ran while one was open for 1% of the time, Pallas kernels for 0%

profile of v1, /device:TPU:0, one launch (start us, length us, event | category | flops | bytes accessed | tf_op | source)
XLA Modules:
  0.0 760.7 jit_solution(5567444273819618124)
XLA Ops:
  8.4 1.5 fusion.14
  9.9 2.4 fusion.10
  12.3 2.7 fusion.16
  15.0 1.5 fusion.18
  16.5 1.5 fusion.20
  18.1 1.6 fusion.22
  19.6 1.6 fusion.24
  21.2 1.6 fusion.12
  23.3 80.8 %reduce-scatter.2.cloned.1.call-done = bf16[2,768,768]{2,1,0:T(8,128)(2,1)} async-done(((bf16[8,768,768]{2,1,0:T(8,128)(2,1)}), bf16[2,768,768]{2,1,0:T(8,128)(2,1)}) %reduce-scatter.2.cloned.1.call-update) | async-done | bytes 2359312 | tf_op jit(solution)/shard_map/reduce_scatter | solution.py:53
  104.1 2.2 convert_element_type.40
  106.3 1.5 collective-permute-start
  107.8 102.1 %collective-permute-done = f32[2,768,768]{2,1,0:T(8,128)S(1)} collective-permute-done((f32[2,768,768]{2,1,0:T(8,128)S(1)}, f32[2,768,768]{2,1,0:T(8,128)S(1)}, u32[]{:S(2)}, u32[]{:S(2)}) %collective-permute-start) | collective-permute-done | bytes 4718624 | tf_op jit(solution)/shard_map/ppermute | solution.py:17
  210.5 1.5 collective-permute-start.1
  212.0 101.2 %collective-permute-done.1 = f32[2,768,768]{2,1,0:T(8,128)S(1)} collective-permute-done((f32[2,768,768]{2,1,0:T(8,128)S(1)}, f32[2,768,768]{2,1,0:T(8,128)S(1)}, u32[]{:S(2)}, u32[]{:S(2)}) %collective-permute-start.1) | collective-permute-done | bytes 4718624 | tf_op jit(solution)/shard_map/ppermute | solution.py:17
  313.2 2.7 add.43
  315.9 2.4 collective-permute-start.2
  318.8 201.2 %collective-permute-done.2 = f32[2,768,768]{2,1,0:T(8,128)} collective-permute-done((f32[2,768,768]{2,1,0:T(8,128)}, f32[2,768,768]{2,1,0:T(8,128)}, u32[]{:S(2)}, u32[]{:S(2)}) %collective-permute-start.2) | collective-permute-done | bytes 4718624 | tf_op jit(solution)/shard_map/ppermute | solution.py:17
  520.0 5.4 select_reduce_fusion
  525.5 2.9 abs_reduce_fusion
  528.4 14.5 %fusion.2 = f32[2,768,768]{2,1,0:T(8,128)S(1)} fusion(f32[2,768,768]{2,1,0:T(8,128)} %get-tuple-element.8, f32[2]{0:T(128)S(1)} %reduce_max.9, f32[768,768]{1,0:T(8,128)S(1)} %fusion.26), kind=kOutput, calls=%fused_computation.10 | convolution fusion | flops 10872815616 | bytes 11796488 | tf_op jit(solution)/shard_map/kij,kjl->kil/dot_general | solution.py:67
  543.0 12.7 %multiply_subtract_fusion.2 = f32[2,768,768]{2,1,0:T(8,128)S(1)} fusion(f32[2]{0:T(128)S(1)} %reduce_max.9, f32[768,768]{1,0:T(8,128)S(1)} %fusion.26, f32[2,768,768]{2,1,0:T(8,128)S(1)} %fusion.2), kind=kOutput, calls=%fused_computation.4 | convolution fusion | flops 10876354560 | bytes 11796488 | tf_op jit(solution)/shard_map/kij,kjl->kil/dot_general | solution.py:68
  555.7 12.1 %fusion.40 = f32[2,768,768]{2,1,0:T(8,128)S(1)} fusion(f32[2,768,768]{2,1,0:T(8,128)S(1)} %bitcast.80, f32[2,768,768]{2,1,0:T(8,128)S(1)} %multiply_subtract_fusion.2), kind=kOutput, calls=%fused_computation.66 | convolution fusion | flops 10871635968 | bytes 14155776 | tf_op jit(solution)/shard_map/kij,kjl->kil/dot_general | solution.py:67
  567.8 12.7 %multiply_subtract_fusion.1 = f32[2,768,768]{2,1,0:T(8,128)S(1)} fusion(f32[2,768,768]{2,1,0:T(8,128)S(1)} %multiply_subtract_fusion.2, f32[2,768,768]{2,1,0:T(8,128)S(1)} %fusion.40), kind=kOutput, calls=%fused_computation.3 | convolution fusion | flops 10873995264 | bytes 14155776 | tf_op jit(solution)/shard_map/kij,kjl->kil/dot_general | solution.py:68
  580.5 12.3 %fusion.41 = f32[2,768,768]{2,1,0:T(8,128)S(1)} fusion(f32[2,768,768]{2,1,0:T(8,128)S(1)} %bitcast.80, f32[2,768,768]{2,1,0:T(8,128)S(1)} %multiply_subtract_fusion.1), kind=kOutput, calls=%fused_computation.67 | convolution fusion | flops 10871635968 | bytes 14155776 | tf_op jit(solution)/shard_map/kij,kjl->kil/dot_general | solution.py:67
  592.8 12.5 %multiply_subtract_fusion = f32[2,768,768]{2,1,0:T(8,128)S(1)} fusion(f32[2,768,768]{2,1,0:T(8,128)S(1)} %multiply_subtract_fusion.1, f32[2,768,768]{2,1,0:T(8,128)S(1)} %fusion.41), kind=kOutput, calls=%fused_computation.2 | convolution fusion | flops 10873995264 | bytes 14155776 | tf_op jit(solution)/shard_map/kij,kjl->kil/dot_general | solution.py:68
  605.4 2.6 slice_select_fusion
  609.7 1.9 constant_dynamic-slice_fusion
  611.6 91.8 %all-reduce.3.cloned.1.call-done = (f32[1,768,768]{2,1,0:T(8,128)}, f32[1,768,768]{2,1,0:T(8,128)}) async-done(((f32[1,768,768]{2,1,0:T(8,128)}, f32[1,768,768]{2,1,0:T(8,128)}), (f32[1,768,768]{2,1,0:T(8,128)}, f32[1,768,768]{2,1,0:T(8,128)})) %all-reduce.3.cloned.1.call-update) | async-done | bytes 4718608 | tf_op jit(solution)/shard_map/psum | solution.py:30
  703.4 2.1 fusion.8
  705.5 14.5 %all-gather.5.cloned.1.call-done = bf16[6,768,768]{2,1,0:T(8,128)(2,1)} async-done(((bf16[6,96,768]{2,1,0:T(8,128)(2,1)}), bf16[6,768,768]{2,1,0:T(8,128)(2,1)}) %all-gather.5.cloned.1.call-update) | async-done | bytes 7077904 | tf_op jit(solution)/shard_map/all_gather | solution.py:77
  720.0 23.5 %all-gather.3.cloned.1.call-done = f32[8,96,768]{2,1,0:T(8,128)} async-done(((f32[2,96,768]{2,1,0:T(8,128)}), f32[8,96,768]{2,1,0:T(8,128)}) %all-gather.3.cloned.1.call-update) | async-done | bytes 2359312 | tf_op jit(solution)/shard_map/all_gather | solution.py:70
  743.6 6.7 fusion.42
  (37 shorter events, 7.1 us)
Async XLA Ops:
  7.4 1.0 copy-start
  7.4 7.6 %copy-start.6 = (bf16[5,256,768]{2,1,0:T(8,128)(2,1)S(1)}, bf16[5,256,768]{2,1,0:T(8,128)(2,1)}, u32[]{:S(2)}) copy-start(bf16[5,256,768]{2,1,0:T(8,128)(2,1)} %param.7) | copy-start | bytes 5898244
  7.4 96.7 %reduce-scatter.2.cloned.1.call-start = ((), (), s32[]{:S(2)}) async-start(), calls=%async_computation.1 | async-start | bytes 11796480 | tf_op jit(solution)/shard_map/reduce_scatter | solution.py:53
  12.3 8.9 %copy-start.5 = (bf16[32,768]{1,0:T(8,128)(2,1)S(1)}, bf16[32,768]{1,0:T(8,128)(2,1)}, u32[]{:S(2)}) copy-start(bf16[32,768]{1,0:T(8,128)(2,1)} %param.9) | copy-start | bytes 147460
  22.8 680.6 %all-reduce.3.cloned.1.call-start = ((), (), s32[]{:S(2)}) async-start(), calls=%async_computation.4 | async-start | bytes 9437184 | tf_op jit(solution)/shard_map/psum | solution.py:30
  104.1 105.8 %copy-start.3 = (bf16[2,768,768]{2,1,0:T(8,128)(2,1)S(1)}, bf16[2,768,768]{2,1,0:T(8,128)(2,1)}, u32[]{:S(2)}) copy-start(bf16[2,768,768]{2,1,0:T(8,128)(2,1)} %reduce-scatter.2.cloned.1.call-done) | copy-start | bytes 7077892
  106.3 103.6 %collective-permute-start = (f32[2,768,768]{2,1,0:T(8,128)S(1)}, f32[2,768,768]{2,1,0:T(8,128)S(1)}, u32[]{:S(2)}, u32[]{:S(2)}) collective-permute-start(f32[2,768,768]{2,1,0:T(8,128)S(1)} %convert_element_type.40), channel_id=1, source_target_pairs={{0,1},{1,0},{2,3},{3,2},{4,5},{5,4},{6,7},{7,6},{8,9},{9,8},{10,11... | collective-permute-start | bytes 14155784 | tf_op jit(solution)/shard_map/ppermute | solution.py:17
  210.5 102.7 %collective-permute-start.1 = (f32[2,768,768]{2,1,0:T(8,128)S(1)}, f32[2,768,768]{2,1,0:T(8,128)S(1)}, u32[]{:S(2)}, u32[]{:S(2)}) collective-permute-start(f32[2,768,768]{2,1,0:T(8,128)S(1)} %convert_add_fusion), channel_id=1, source_target_pairs={{0,2},{1,3},{2,0},{3,1},{4,6},{5,7},{6,4},{7,5},{8,10},{9,11},{10,... | collective-permute-start | bytes 14155784 | tf_op jit(solution)/shard_map/ppermute | solution.py:17
  315.9 204.1 %collective-permute-start.2 = (f32[2,768,768]{2,1,0:T(8,128)}, f32[2,768,768]{2,1,0:T(8,128)}, u32[]{:S(2)}, u32[]{:S(2)}) collective-permute-start(f32[2,768,768]{2,1,0:T(8,128)} %add.43), channel_id=1, source_target_pairs={{0,4},{1,5},{2,6},{3,7},{4,0},{5,1},{6,2},{7,3},{8,12},{9,13},{10,... | collective-permute-start | bytes 14155784 | tf_op jit(solution)/shard_map/ppermute | solution.py:17
  528.4 27.3 %slice-start = ((s8[4718592]{0:T(1024)(128)(4,1)}), s8[4194304]{0:T(1024)(128)(4,1)S(1)}, s32[]{:S(2)}) async-start(s8[4718592]{0:T(1024)(128)(4,1)} %bitcast.79), calls=%async_computation.5 | async-start | bytes 8388608
  543.0 12.8 %slice-start.1 = ((s8[4718592]{0:T(1024)(128)(4,1)}), s8[524288]{0:T(1024)(128)(4,1)S(1)}, s32[]{:S(2)}) async-start(s8[4718592]{0:T(1024)(128)(4,1)} %bitcast.79), calls=%async_computation.6 | async-start | bytes 1048576
  605.4 3.7 copy-start.2
  609.0 111.0 %all-gather.5.cloned.1.call-start = ((), (), s32[]{:S(2)}) async-start(), calls=%async_computation.3 | async-start | bytes 7962624 | tf_op jit(solution)/shard_map/all_gather | solution.py:77
  609.6 134.0 %all-gather.3.cloned.1.call-start = ((), (), s32[]{:S(2)}) async-start(), calls=%async_computation.2 | async-start | bytes 2949120 | tf_op jit(solution)/shard_map/all_gather | solution.py:70
  705.5 46.7 %copy-start.4 = (f32[6,96,192]{2,1,0:T(8,128)S(1)}, f32[6,96,192]{2,1,0:T(8,128)}, u32[]{:S(2)}) copy-start(f32[6,96,192]{2,1,0:T(8,128)} %param.11) | copy-start | bytes 1327108
  743.6 9.5 %copy-start.1 = (bf16[256,768]{1,0:T(8,128)(2,1)S(1)}, bf16[256,768]{1,0:T(8,128)(2,1)}, u32[]{:S(2)}) copy-start(bf16[256,768]{1,0:T(8,128)(2,1)} %param.6) | copy-start | bytes 1179652
Sparse Core Ops, SparseCore 0:
  22.9 81.1 reduce-scatter.1
  609.2 94.2 all-reduce.2
Sparse Core Ops, SparseCore 1:
  611.7 108.3 all-gather.4
  721.5 22.1 all-gather.2
